TPU v7x, 128 devices: a whole 4x4x4 slice. The times are simulated.
128 devices in a mesh: req: 16 (over z, y), mlp: 8 (over x, core).
Axes of the slice: x: 4, y: 4, z: 4, core: 2. Of those that a mesh axis runs over, the one named last changes fastest.
Arguments:
- hidden: bfloat16 [8192, 3584], P('req', 'mlp'), may hold values from -6 to 6
- query_heads: bfloat16 [8192, 3584], P('req', 'mlp'), may hold values from -4 to 4
- key_heads: bfloat16 [8192, 3584], P('req', 'mlp'), may hold values from -4 to 4
- value_heads: bfloat16 [8192, 3584], P('req', 'mlp'), may hold values from -6 to 6
- segment_ids: int32 [8192], P('req'), may hold values from 0 to 63, never falling along the last dimension, each value on 1 to 1024 neighbouring positions
- page_table: int32 [16, 32], P('req'), may hold values from 0 to 31, each once within a row
- mamba_conv_input: bfloat16 [8192, 7168], P('req', 'mlp'), may hold values from -6 to 6
- mamba_output_gate: bfloat16 [8192, 7168], P('req', 'mlp'), may hold values from -6 to 6
- state_input_projection: bfloat16 [8192, 128], P('req'), may hold values from -6 to 6
- state_output_projection: bfloat16 [8192, 128], P('req'), may hold values from -6 to 6
- discrete_step_size: float32 [8192, 112], P('req', 'mlp'), may hold values from 0.24 to 100, as said below
- head_decay_rate: float32 [112], P('mlp'), may hold values from 0.00024414062 to 0.05, as said below
- skip_gain: float32 [112], P('mlp'), may hold values from 0.5 to 2
- mamba_gated_norm_gain: float32 [7168], P('mlp'), may hold values from 0.1 to 1.9
- attn_proj: bfloat16 [3584, 3584], P('mlp'), may hold values from -0.09375 to 0.09375
- mamba_output_projection: bfloat16 [7168, 3584], P('mlp'), may hold values from -0.0625 to 0.0625
- mlp_norm_gain: float32 [3584], replicated, may hold values from 0.1 to 1.9
- gate_proj: bfloat16 [3584, 7168], P('req', 'mlp'), may hold values from -0.09375 to 0.09375
- up_proj: bfloat16 [3584, 7168], P('req', 'mlp'), may hold values from -0.09375 to 0.09375
- down_proj: bfloat16 [7168, 3584], P('mlp', 'req'), may hold values from -0.0625 to 0.0625
- next_norm_gain: float32 [3584], P('mlp'), may hold values from 0.1 to 1.9
Outputs:
- new_hidden: bfloat16 [8192, 3584], P('req', 'mlp')
- next_normed: bfloat16 [8192, 3584], P('req', 'mlp')
- kv_cache: bfloat16 [2, 16, 512, 3584], P(None, 'mlp', 'req')
Inputs may be any that keep to these rules, and one draw needn't show every extreme that they name: `segment_ids`: prompt ids never fall along the stream; a prompt has 1 to 1024 tokens and one has exactly 1024. `page_table`: each request group's row names every page of its pool once. `discrete_step_size`: Positive. `head_decay_rate`: Positive.
All inputs are finite; a program needn't handle non-finite values.
Results may differ from a plain program's by a relative error of at most 0.006.
Values may be sent and summed in bfloat16 or wider, within the bound.
No kernel may reach another device: no remote copies, remote signals or barrier semaphores. Data moves between devices by JAX's collectives and lax.ppermute only.
A program may use at most 128 MiB of HBM per device.

v0:
```python
import math
import jax
import jax.numpy as jnp
from jax import lax
from jax.sharding import PartitionSpec as P

HD = 224
MAMBA_HEAD_COUNT = 112
MAMBA_HEAD_SIZE = 64
STATE_SIZE = 64
STATE_GROUPS = 2
REACH = 2
PAGE = 16
EPSILON = 1e-05
exact_mode = lax.Precision.HIGHEST


def from_behind(value, axis, steps):
    count = lax.axis_size(axis)
    leading, last = (max(0, -steps), min(count, count - steps))
    return lax.ppermute(value, axis, [(source, source + steps) for source in range(leading, last)])


def entering(x, axis, combine, identity):
    devices, mine = (lax.axis_size(axis), lax.axis_index(axis))
    everything = jax.tree.map(lambda part: lax.all_gather(part, axis), x)
    start = jax.tree.map(
        lambda part, zero: jnp.broadcast_to(jnp.asarray(zero, part.dtype), part.shape), x, identity
    )

    def step(k, before):
        reached = k < mine
        new = combine(before, jax.tree.map(lambda part: part[k], everything))
        return jax.tree.map(lambda a, b: jnp.where(reached, a, b), new, before)

    return lax.fori_loop(0, devices, step, start)


def attend_rows(
    query_rows, segment_rows, pos_rows, all_keys, all_values, key_segs, key_pos, head_count
):
    row_total = query_rows.shape[0]
    key_total = all_keys.shape[0]
    query_split = query_rows.reshape(row_total, head_count, HD)
    key_split = all_keys.reshape(key_total, head_count, HD)
    value_split = all_values.reshape(key_total, head_count, HD)
    scores = jnp.einsum(
        "qhd,khd->hqk", query_split, key_split, preferred_element_type=jnp.float32
    ) * (1.0 / math.sqrt(HD))
    allowed = (segment_rows[:, None] == key_segs[None, :]) & (key_pos[None, :] <= pos_rows[:, None])
    scores = jnp.where(allowed[None, :, :], scores, -jnp.inf)
    top_score = jnp.max(scores, axis=2, keepdims=True)
    raised = jnp.exp(scores - top_score)
    weights = (raised / jnp.sum(raised, axis=2, keepdims=True)).astype(jnp.bfloat16)
    summed = jnp.einsum("hqk,khd->qhd", weights, value_split, preferred_element_type=jnp.float32)
    return summed.astype(jnp.bfloat16).reshape(row_total, head_count * HD)


def block_contributions(
    input_token_rows,
    input_proj_rows,
    output_proj_rows,
    step_size_rows,
    head_decay_rate,
    segment_rows,
    segment_prior_state,
    group_index,
    head_width,
):
    row_count = input_token_rows.shape[0]
    head_count = step_size_rows.shape[1]
    input_float = input_token_rows.astype(jnp.float32).reshape(row_count, head_count, head_width)
    b_float = input_proj_rows.astype(jnp.float32)
    c_float = output_proj_rows.astype(jnp.float32)
    running = jnp.cumsum(-step_size_rows * head_decay_rate[None, :], axis=0)
    positions = jnp.arange(row_count, dtype=jnp.int32)
    live = (segment_rows[:, None] == segment_rows[None, :]) & (
        positions[:, None] >= positions[None, :]
    )
    spread = running.T[:, :, None] - running.T[:, None, :]
    mixing = jnp.exp(jnp.where(live[None, :, :], spread, -1e30))
    inner = jnp.einsum("tgn,ugn->gtu", c_float, b_float, precision=exact_mode)
    driven = input_float * step_size_rows[:, :, None]
    local_output = jnp.einsum(
        "htu,uhp->thp", mixing * inner[group_index], driven, precision=exact_mode
    )
    b_per_head = b_float[:, group_index, :]
    output_proj_per_head = c_float[:, group_index, :]
    tail_rows = segment_rows == segment_rows[row_count - 1]
    tail_gain = jnp.where(
        tail_rows[:, None], jnp.exp(running[row_count - 1][None, :] - running), 0.0
    )
    state_local_part = jnp.einsum(
        "uh,uhp,uhn->hpn", tail_gain, driven, b_per_head, precision=exact_mode
    )
    decay_cumulative = jnp.where(
        segment_rows[row_count - 1] == segment_prior_state, jnp.exp(running[row_count - 1]), 0.0
    )
    entry_weighting = jnp.where(
        (segment_rows == segment_prior_state)[:, None], jnp.exp(running), 0.0
    )
    return (
        local_output,
        decay_cumulative,
        state_local_part,
        entry_weighting,
        input_float,
        output_proj_per_head,
    )


def finish(local_output, entry_weighting, input_float, output_proj_per_head, carry_in, skip_gain):
    carried = jnp.einsum("hpn,thn->thp", carry_in, output_proj_per_head, precision=exact_mode)
    result = (
        local_output
        + entry_weighting[:, :, None] * carried
        + skip_gain[None, :, None] * input_float
    )
    return result.reshape(result.shape[0], result.shape[1] * result.shape[2])


def merge_states(earlier, later):
    decay_early, state_early = earlier
    decay_late, state_late = later
    return (decay_early * decay_late, decay_late[:, None, None] * state_early + state_late)


def body(
    hidden,
    query_heads,
    key_heads,
    value_heads,
    segment_ids,
    page_table,
    mamba_conv_input,
    mamba_output_gate,
    state_input_projection,
    state_output_projection,
    discrete_step_size,
    head_decay_rate,
    skip_gain,
    mamba_gated_norm_gain,
    attn_proj,
    mamba_output_projection,
    mlp_norm_gain,
    gate_proj,
    up_proj,
    down_proj,
    next_norm_gain,
):
    row_count = query_heads.shape[0]
    head_count = query_heads.shape[1] // HD
    lane_count = hidden.shape[1]
    owner_index = lax.axis_index("req")
    column = lax.axis_index("mlp")
    first_row = owner_index * row_count
    lead_rows = REACH * row_count
    shifted_ids = segment_ids + 1
    key_parts = []
    value_parts = []
    segment_parts = []
    for distance in range(REACH, 0, -1):
        moved_ids = from_behind(shifted_ids, "req", distance)
        segment_parts.append(moved_ids - 1)
        moved_keys, moved_values = from_behind((key_heads, value_heads), "req", distance)
        key_parts.append(moved_keys)
        value_parts.append(moved_values)
    key_segs = jnp.concatenate(segment_parts + [segment_ids], axis=0)
    key_pos = first_row - lead_rows + jnp.arange(lead_rows + row_count, dtype=jnp.int32)
    segment_prior_state = segment_parts[-1][row_count - 1]
    all_keys = jnp.concatenate(key_parts + [key_heads], axis=0)
    all_values = jnp.concatenate(value_parts + [value_heads], axis=0)
    block_rows = min(row_count, 512)

    def one_block(block_index):
        first_local = block_index * block_rows
        pos_rows = first_row + first_local + jnp.arange(block_rows, dtype=jnp.int32)
        return attend_rows(
            query_heads, segment_ids, pos_rows, all_keys, all_values, key_segs, key_pos, head_count
        )

    attended = lax.map(one_block, jnp.arange(row_count // block_rows, dtype=jnp.int32)).reshape(
        row_count, head_count * HD
    )
    page_count = page_table.shape[1]
    key_pages = (
        key_heads.reshape(page_count, PAGE, head_count, HD)
        .transpose(2, 0, 1, 3)
        .reshape(head_count, page_count, PAGE * HD)
    )
    value_pages = (
        value_heads.reshape(page_count, PAGE, head_count, HD)
        .transpose(2, 0, 1, 3)
        .reshape(head_count, page_count, PAGE * HD)
    )
    stacked = jnp.stack([key_pages, value_pages])
    kv_cache = jnp.zeros_like(stacked).at[:, :, page_table[0]].set(stacked)
    mamba_heads = discrete_step_size.shape[1]
    group_values = MAMBA_HEAD_COUNT // STATE_GROUPS
    b_groups = state_input_projection.reshape(row_count, STATE_GROUPS, STATE_SIZE)
    c_groups = state_output_projection.reshape(row_count, STATE_GROUPS, STATE_SIZE)
    group_index = jnp.arange(mamba_heads, dtype=jnp.int32) % STATE_GROUPS
    (
        local_output,
        decay_cumulative,
        state_local_part,
        entry_weighting,
        input_float,
        output_proj_per_head,
    ) = block_contributions(
        mamba_conv_input,
        b_groups,
        c_groups,
        discrete_step_size,
        head_decay_rate,
        segment_ids,
        segment_prior_state,
        group_index,
        MAMBA_HEAD_SIZE,
    )
    unused_decay, carry_in = entering(
        (decay_cumulative, state_local_part),
        "req",
        merge_states,
        (jnp.ones_like(decay_cumulative), jnp.zeros_like(state_local_part)),
    )
    mamba_output = finish(
        local_output, entry_weighting, input_float, output_proj_per_head, carry_in, skip_gain
    )
    gated_output = mamba_output * jax.nn.silu(mamba_output_gate.astype(jnp.float32))
    grouped_values = gated_output.reshape(
        row_count, mamba_heads // STATE_GROUPS, STATE_GROUPS, MAMBA_HEAD_SIZE
    )
    group_squares = jnp.sum(grouped_values * grouped_values, axis=(1, 3))
    running_totals = lax.psum(group_squares, "mlp")
    inverse_group = lax.rsqrt(running_totals / (group_values * MAMBA_HEAD_SIZE) + EPSILON)
    mnormed = (
        (grouped_values * inverse_group[:, None, :, None]).reshape(
            row_count, mamba_heads * MAMBA_HEAD_SIZE
        )
        * mamba_gated_norm_gain[None, :]
    ).astype(jnp.bfloat16)
    projected = jnp.dot(attended, attn_proj, preferred_element_type=jnp.float32) + jnp.dot(
        mnormed, mamba_output_projection, preferred_element_type=jnp.float32
    )
    width_total = projected.shape[1]
    offset = column * lane_count
    own_part = lax.dynamic_slice_in_dim(projected, offset, lane_count, 1) + hidden.astype(
        jnp.float32
    )
    mixed_rows = lax.psum(lax.dynamic_update_slice_in_dim(projected, own_part, offset, 1), "mlp")
    mixed_share = lax.dynamic_slice_in_dim(mixed_rows, offset, lane_count, 1)
    inverse_root_mean = lax.rsqrt(jnp.mean(mixed_rows * mixed_rows, axis=1) + EPSILON)
    normed = (mixed_rows * inverse_root_mean[:, None] * mlp_norm_gain[None, :]).astype(jnp.bfloat16)
    gate_act = jnp.dot(
        normed,
        lax.all_gather(gate_proj, "req", axis=0, tiled=True),
        preferred_element_type=jnp.float32,
    )
    up_act = jnp.dot(
        normed,
        lax.all_gather(up_proj, "req", axis=0, tiled=True),
        preferred_element_type=jnp.float32,
    )
    latent_activation = (jax.nn.silu(gate_act) * up_act).astype(jnp.bfloat16)
    partial_value = jnp.dot(
        latent_activation,
        lax.all_gather(down_proj, "req", axis=1, tiled=True),
        preferred_element_type=jnp.float32,
    )
    mlp_share = lax.psum_scatter(partial_value, "mlp", scatter_dimension=1, tiled=True)
    new_hidden = (mixed_share + mlp_share).astype(jnp.bfloat16)
    widened = new_hidden.astype(jnp.float32)
    total_sq = lax.psum(jnp.sum(widened * widened, axis=1), "mlp")
    next_normed = (
        widened * lax.rsqrt(total_sq / width_total + EPSILON)[:, None] * next_norm_gain[None, :]
    ).astype(jnp.bfloat16)
    return (new_hidden, next_normed, kv_cache)


def solution(mesh):
    return jax.shard_map(
        body,
        mesh=mesh,
        in_specs=(
            P("req", "mlp"),
            P("req", "mlp"),
            P("req", "mlp"),
            P("req", "mlp"),
            P("req"),
            P("req", None),
            P("req", "mlp"),
            P("req", "mlp"),
            P("req", None),
            P("req", None),
            P("req", "mlp"),
            P("mlp"),
            P("mlp"),
            P("mlp"),
            P("mlp", None),
            P("mlp", None),
            P(),
            P("req", "mlp"),
            P("req", "mlp"),
            P("mlp", "req"),
            P("mlp"),
        ),
        out_specs=(P("req", "mlp"), P("req", "mlp"), P(None, "mlp", "req", None)),
        check_vma=False,
    )
```

profile of v0, /device:TPU:0, one launch (start us, length us, event | category | flops | bytes accessed | tf_op | source)
XLA Modules:
  0.0 616.1 jit_solution(2052999723825984348)
XLA Ops:
  8.7 3.6 collective-permute-start.3
  16.9 2.5 copy.75
  25.6 3.5 fusion.22
  29.2 5.4 collective-permute-start.2
  34.6 4.1 collective-permute-start.4
  38.7 4.3 collective-permute-start.5
  43.0 4.0 collective-permute-start
  47.0 3.6 collective-permute-start.1
  56.1 8.8 %gather_fusion = f32[14,512,512]{2,1,0:T(8,128)} fusion(f32[2,512,512]{2,1,0:T(8,128)} %fusion.59, s32[1024]{0:T(1024)} %copy-done.13), kind=kCustom, calls=%fused_computation | custom fusion | bytes 29360184 | tf_op jit(solution)/shard_map/gather | solution.py:85
  69.6 39.1 %all-gather.1 = f32[16,1,14]{2,1,0:T(1,128)S(1)} all-gather(f32[1,1,14]{2,1,0:T(1,128)S(1)} %bitcast.114), channel_id=1, replica_groups=mesh['req'=16,'mlp'=8] {'req'}, dimensions={0}, use_global_device_ids=true | all-gather | bytes 952 | tf_op jit(solution)/shard_map/all_gather | solution.py:26
  108.7 2.5 pad_maximum_fusion.1
  111.3 2.3 pad_maximum_fusion
  113.6 4.1 fusion.58
  117.7 6.2 %fusion.30 = bf16[2,224,512]{2,1,0:T(8,128)(2,1)} fusion(bf16[1536,2,224]{0,2,1:T(8,128)(2,1)} %bitcast.105, f32[2,512]{1,0:T(2,128)S(1)} %fusion.58, pred[512,1536]{0,1:T(8,128)(4,1)} %compare_and_fusion, bf16[1536,2,224]{0,2,1:T(8,128)(2,1)} %bitcast.104, bf16[512,2,224]{0,2,1:T(8,128)(2,1)} %bitcast.116), kind=kOutput, calls=%fused_computation.49 | convolution fusion | flops 1417382400 | bytes 4460544 | tf_op jit(solution)/shard_map/while/body/eval_jaxpr/hqk,khd->qhd/dot_general | solution.py:55
  123.9 43.8 %while.18 = (s32[]{:T(128)}, f32[14,64,64]{2,1,0:T(8,128)}, s32[]{:T(128)}, f32[16,14]{1,0:T(8,128)S(1)}, f32[16,14,64,64]{3,2,1,0:T(8,128)}, /*index=5*/s32[]{:T(128)}, s32[]{:T(128)}) while((s32[]{:T(128)}, f32[14,64,64]{2,1,0:T(8,128)}, s32[]{:T(128)}, f32[16,14]{1,0:T(8,128)S(1)}, f32[16,14,64,64]{3,2,1,0:T(8,128)}, ...), condition=%wide.region_5.6_spmd.clone, body=%wide.region_4.5_spmd.clone.sunk | while | flops 229380 | bytes 688401 | solution.py:36
  136.9 2.0 fusion.75
  138.9 2.0 fusion.75
  141.0 2.0 fusion.75
  143.0 2.0 fusion.75
  145.1 2.0 fusion.75
  147.1 2.0 fusion.75
  149.2 2.0 fusion.75
  151.2 2.0 fusion.75
  153.3 2.0 fusion.75
  155.3 2.0 fusion.75
  167.7 2.3 fusion.37
  170.0 20.4 %fusion.21 = f32[512,14,64]{0,2,1:T(8,128)} fusion(f32[14,512,64]{1,2,0:T(8,128)S(1)} %fusion.37, f32[512,14,64]{0,2,1:T(8,128)S(1)} %bitcast.98, f32[14,512,512]{2,1,0:T(8,128)} %gather_fusion, f32[14,512]{1,0:T(8,128)S(1)} %bitcast.111, pred[512,512]{1,0:T(8,128)(4,1)S(1)} %copy-done.9, f32[14]{0:T(128)S(1)} %copy-done.18, f32[512,14]{0,1:T(8,128)S(1)} %copy-done.12, ...), kind=kOutput, calls=%fused_computation.38 | convolution fusion | flops 2831876096 | bytes 20533304 | tf_op jit(solution)/shard_map/htu,uhp->thp/dot_general | solution.py:84
  190.5 2.8 copy.80
  193.2 3.4 fusion.56
  196.7 2.8 copy.81
  201.1 12.4 %psum.21 = f32[512,2]{0,1:T(2,128)S(1)} all-reduce(f32[512,2]{0,1:T(2,128)S(1)} %reduce_sum.38), channel_id=1, replica_groups=mesh['req'=16,'mlp'=8] {'mlp'}, use_global_device_ids=true, to_apply=%region_7.8 | all-reduce | flops 1024 | bytes 8192 | tf_op jit(solution)/shard_map/psum | solution.py:235
  215.0 2.7 copy.82
  217.8 8.2 %fusion.35 = f32[512,3584]{1,0:T(8,128)S(1)} fusion(bf16[896,3584]{1,0:T(8,128)(2,1)} %param.38, f32[512,896]{1,0:T(8,128)} %copy.82, f32[896]{0:T(1024)S(1)} %copy-done.17, f32[512,896]{1,0:T(8,128)} %copy.80, bf16[512,896]{1,0:T(8,128)(2,1)} %param.30), kind=kOutput, calls=%fused_computation.57 | convolution fusion | flops 3292463104 | bytes 18353664 | tf_op jit(solution)/shard_map/dot_general | solution.py:243
  226.0 2.2 convolution_add_fusion
  228.2 3.0 copy-done.2
  231.5 5.8 dynamic_update_slice.6
  239.3 88.7 %all-reduce.2.cloned.1.call-done = f32[512,3584]{1,0:T(8,128)} async-done(((f32[512,3584]{1,0:T(8,128)}), f32[512,3584]{1,0:T(8,128)}) %all-reduce.2.cloned.1.call-update) | async-done | bytes 7340048 | tf_op jit(solution)/shard_map/psum | solution.py:251
  328.1 3.6 multiply_reduce_fusion
  331.7 60.3 %all-gather.7.cloned.1.call-done = bf16[3584,896]{1,0:T(8,128)(2,1)} async-done(((bf16[224,896]{1,0:T(8,128)(2,1)}), bf16[3584,896]{1,0:T(8,128)(2,1)}) %all-gather.7.cloned.1.call-update) | async-done | bytes 6422544 | tf_op jit(solution)/shard_map/all_gather | solution.py:257
  392.0 8.4 %fusion.57 = f32[512,896]{1,0:T(8,128)S(1)} fusion(bf16[3584,896]{1,0:T(8,128)(2,1)} %all-gather.7.cloned.1.call-done, f32[512,3584]{1,0:T(8,128)} %all-reduce.2.cloned.1.call-done, f32[3584]{0:T(1024)S(1)} %copy-done.16, f32[512]{0:T(512)S(1)} %add_rsqrt_fusion.2), kind=kOutput, calls=%fused_computation.98 | convolution fusion | flops 3293839360 | bytes 15613952 | tf_op jit(solution)/shard_map/dot_general | solution.py:255
  400.5 55.1 %all-gather.11.cloned.1.call-done = bf16[896,3584]{0,1:T(8,128)(2,1)} async-done(((bf16[896,224]{0,1:T(8,128)(2,1)}), bf16[896,3584]{0,1:T(8,128)(2,1)}) %all-gather.11.cloned.1.call-update) | async-done | bytes 6422544 | tf_op jit(solution)/shard_map/all_gather | solution.py:268
  455.6 63.6 %all-gather.9.cloned.1.call-done = bf16[3584,896]{1,0:T(8,128)(2,1)} async-done(((bf16[224,896]{1,0:T(8,128)(2,1)}), bf16[3584,896]{1,0:T(8,128)(2,1)}) %all-gather.9.cloned.1.call-update) | async-done | bytes 6422544 | tf_op jit(solution)/shard_map/all_gather | solution.py:262
  519.2 17.7 %convolution_bitcast_fusion = f32[3584,512]{1,0:T(8,128)} fusion(bf16[896,3584]{0,1:T(8,128)(2,1)} %all-gather.11.cloned.1.call-done, f32[512,896]{1,0:T(8,128)S(1)} %fusion.57, bf16[3584,896]{1,0:T(8,128)(2,1)} %all-gather.9.cloned.1.call-done, f32[512,3584]{1,0:T(8,128)} %all-reduce.2.cloned.1.call-done, f32[3584]{0:T(1024)S(1)} %copy-done.16, ...), kind=kOutput, calls=%fused_computation.19 | convolution fusion | flops 6584926208 | bytes 29376512
  542.5 2.6 scatter_fusion
  546.0 38.0 %reduce-scatter.4.cloned.1.call-done = f32[448,512]{1,0:T(8,128)} async-done(((f32[3584,512]{1,0:T(8,128)}), f32[448,512]{1,0:T(8,128)}) %reduce-scatter.4.cloned.1.call-update) | async-done | bytes 917520
  584.1 2.7 copy.96
  586.7 2.8 fusion.31
  589.6 13.2 %psum.23 = f32[512]{0:T(512)S(1)} all-reduce(f32[512]{0:T(512)S(1)} %get-tuple-element.167), channel_id=1, replica_groups=mesh['req'=16,'mlp'=8] {'mlp'}, use_global_device_ids=true, to_apply=%region_12.13 | all-reduce | flops 512 | bytes 4096 | tf_op jit(solution)/shard_map/psum | solution.py:274
  (135 shorter events, 51.3 us)
Async XLA Ops:
  7.2 218.8 %copy-start = (bf16[448,3584]{1,0:T(8,128)(2,1)S(1)}, bf16[448,3584]{1,0:T(8,128)(2,1)}, u32[]{:S(2)}) copy-start(bf16[448,3584]{1,0:T(8,128)(2,1)} %param.37) | copy-start | bytes 9633796
  7.2 116.7 %all-gather.13.cloned.1.call-start = ((), (), s32[]{:S(2)}) async-start(), calls=%async_computation.5 | async-start | bytes 7798784 | tf_op jit(solution)/shard_map/all_gather | solution.py:26
  8.7 12.3 %collective-permute-start.3 = (s32[512]{0:T(512)}, s32[512]{0:T(512)S(1)}, u32[]{:S(2)}, u32[]{:S(2)}) collective-permute-start(s32[512]{0:T(512)} %broadcast_add_fusion.3), channel_id=1, source_target_pairs={{0,8},{8,16},{16,24},{24,32},{32,40},{40,48},{48,56},{56,64},{64,7... | collective-permute-start | bytes 6152 | tf_op jit(solution)/shard_map/ppermute | solution.py:21
  14.5 6.4 %copy-start.13 = (s32[1024]{0:T(1024)}, s32[1024]{0:T(1024)S(1)}, u32[]{:S(2)}) copy-start(s32[1024]{0:T(1024)S(1)} %pad_clamp_fusion) | copy-start | bytes 12292
  19.4 3.4 copy-start.11
  19.4 6.2 copy-start.10
  29.1 298.9 %all-reduce.2.cloned.1.call-start = ((), (), s32[]{:S(2)}) async-start(), calls=%async_computation.1 | async-start | bytes 14680064 | tf_op jit(solution)/shard_map/psum | solution.py:251
  29.2 37.8 %collective-permute-start.2 = (s32[512]{0:T(512)}, s32[512]{0:T(512)}, u32[]{:S(2)}, u32[]{:S(2)}) collective-permute-start(s32[512]{0:T(512)} %broadcast_add_fusion.3), channel_id=1, source_target_pairs={{0,16},{8,24},{16,32},{24,40},{32,48},{40,56},{48,64},{56,72},{64,... | collective-permute-start | bytes 6152 | tf_op jit(solution)/shard_map/ppermute | solution.py:21
  34.6 74.2 %collective-permute-start.4 = (bf16[512,448]{0,1:T(8,128)(2,1)}, bf16[512,448]{0,1:T(8,128)(2,1)}, u32[]{:S(2)}, u32[]{:S(2)}) collective-permute-start(bf16[512,448]{0,1:T(8,128)(2,1)} %param.25), channel_id=1, source_target_pairs={{0,16},{8,24},{16,32},{24,40},{32,48},{40,56},{48,64},{56,72},{64,... | collective-permute-start | bytes 1376264 | tf_op jit(solution)/shard_map/ppermute | solution.py:21
  38.7 70.1 %collective-permute-start.5 = (bf16[512,448]{0,1:T(8,128)(2,1)}, bf16[512,448]{0,1:T(8,128)(2,1)}, u32[]{:S(2)}, u32[]{:S(2)}) collective-permute-start(bf16[512,448]{0,1:T(8,128)(2,1)} %param.25), channel_id=1, source_target_pairs={{0,8},{8,16},{16,24},{24,32},{32,40},{40,48},{48,56},{56,64},{64,7... | collective-permute-start | bytes 1376264 | tf_op jit(solution)/shard_map/ppermute | solution.py:21
  43.0 68.3 %collective-permute-start = (bf16[512,448]{0,1:T(8,128)(2,1)}, bf16[512,448]{0,1:T(8,128)(2,1)}, u32[]{:S(2)}, u32[]{:S(2)}) collective-permute-start(bf16[512,448]{0,1:T(8,128)(2,1)} %param.26), channel_id=1, source_target_pairs={{0,16},{8,24},{16,32},{24,40},{32,48},{40,56},{48,64},{56,72},{64,... | collective-permute-start | bytes 1376264 | tf_op jit(solution)/shard_map/ppermute | solution.py:21
  47.0 64.3 %collective-permute-start.1 = (bf16[512,448]{0,1:T(8,128)(2,1)}, bf16[512,448]{0,1:T(8,128)(2,1)}, u32[]{:S(2)}, u32[]{:S(2)}) collective-permute-start(bf16[512,448]{0,1:T(8,128)(2,1)} %param.26), channel_id=1, source_target_pairs={{0,8},{8,16},{16,24},{24,32},{32,40},{40,48},{48,56},{56,64},{64,7... | collective-permute-start | bytes 1376264 | tf_op jit(solution)/shard_map/ppermute | solution.py:21
  56.1 13.5 %copy-start.15 = (f32[14]{0:T(128)S(1)}, f32[14]{0:T(128)}, u32[]{:S(2)}) copy-start(f32[14]{0:T(128)} %get-tuple-element.156) | copy-start | bytes 172
  66.9 44.3 %copy-start.6 = (bf16[512,448]{0,1:T(8,128)(2,1)S(1)}, bf16[512,448]{0,1:T(8,128)(2,1)}, u32[]{:S(2)}) copy-start(bf16[512,448]{0,1:T(8,128)(2,1)} %param.26) | copy-start | bytes 1376260
  167.6 2.3 copy-start.3
  167.6 2.3 copy-start.9
  167.6 2.4 copy-start.12
  167.6 2.4 copy-start.18
  213.5 4.2 copy-start.17
  217.8 8.2 %copy-start.8 = (bf16[2,224,512]{2,1,0:T(8,128)(2,1)S(1)}, bf16[2,224,512]{2,1,0:T(8,128)(2,1)}, u32[]{:S(2)}) copy-start(bf16[2,224,512]{2,1,0:T(8,128)(2,1)} %fusion.30) | copy-start | bytes 1376260
  226.0 5.2 copy-start.4
  228.2 3.0 copy-start.2
  237.4 154.6 %all-gather.7.cloned.1.call-start = ((), (), s32[]{:S(2)}) async-start(), calls=%async_computation.2 | async-start | bytes 6823936 | tf_op jit(solution)/shard_map/all_gather | solution.py:257
  238.1 217.5 %all-gather.11.cloned.1.call-start = ((), (), s32[]{:S(2)}) async-start(), calls=%async_computation.4 | async-start | bytes 6823936 | tf_op jit(solution)/shard_map/all_gather | solution.py:268
  238.7 280.5 %all-gather.9.cloned.1.call-start = ((), (), s32[]{:S(2)}) async-start(), calls=%async_computation.3 | async-start | bytes 6823936 | tf_op jit(solution)/shard_map/all_gather | solution.py:262
  239.3 152.7 %copy-start.16 = (f32[3584]{0:T(1024)S(1)}, f32[3584]{0:T(1024)}, u32[]{:S(2)}) copy-start(f32[3584]{0:T(1024)} %param.39) | copy-start | bytes 43012
  239.3 344.8 %reduce-scatter.4.cloned.1.call-start = ((), (), s32[]{:S(2)}) async-start(), calls=%async_computation.6 | async-start | bytes 8257536
  536.9 1.0 copy-start.5
  536.9 1.2 copy-start.7
  540.0 2.0 copy-start.19
  584.1 20.8 %copy-start.14 = (f32[448]{0:T(512)S(1)}, f32[448]{0:T(512)}, u32[]{:S(2)}) copy-start(f32[448]{0:T(512)} %param.43) | copy-start | bytes 5380
  584.1 24.8 %copy-start.1 = (bf16[448,3584]{1,0:T(8,128)(2,1)S(1)}, bf16[448,3584]{1,0:T(8,128)(2,1)}, u32[]{:S(2)}) copy-start(bf16[448,3584]{1,0:T(8,128)(2,1)} %param.37) | copy-start | bytes 9633796
Sparse Core Ops, SparseCore 0:
  29.2 88.2 all-gather.12
  237.5 90.5 all-reduce.1
  330.2 61.7 all-gather.6
  394.0 61.5 all-gather.10
  457.6 61.5 all-gather.8
  537.1 46.9 reduce-scatter.3
where the time goes:
time: 626 us; the launch traced here: 616 us
  waiting for transfers between devices  308 us (49%)
  matrix products  75 us (12%)
  blocking collectives  64.8 us (10%)
  other arithmetic  61.3 us (10%)
  local copies, waits for them, and re-layouts  55 us (9%)
  starting transfers between devices  25.2 us (4%)
  between operations  16.2 us (3%)
  loops' own time  11.1 us (2%)
    psum x1, waiting for transfers between devices, body(): lax.psum(lax.dynamic_update_slice_in_dim(projected, own_part, offset, 1),...  88.7 us
    all_gather x1, waiting for transfers between devices, body(): lax.all_gather(up_proj, 'req', axis=0, tiled=True)  63.6 us
    all_gather x1, waiting for transfers between devices, body(): lax.all_gather(gate_proj, 'req', axis=0, tiled=True)  60.3 us
    all_gather x1, waiting for transfers between devices, body(): lax.all_gather(down_proj, 'req', axis=1, tiled=True)  55.1 us
    unnamed x7, waiting for transfers between devices  39.8 us
    all_gather x1, blocking collectives, entering(): everything = jax.tree.map(lambda part: lax.all_gather(part, axis), x)  39.1 us
    select_n x16, other arithmetic, step(): return jax.tree.map(lambda a, b: jnp.where(reached, a, b), new, before)  32.6 us
    ppermute x6, starting transfers between devices, from_behind(): lax.ppermute(value, axis, [(source, source + steps) for source in range(l...  25 us
  transfers between devices with their start and end apart: 12, of which 5 were waited for; matrix products, arithmetic and copies ran while one was open for 10% of the time, Pallas kernels for 0%

commit v1 on v0

--- a/solution.py
+++ b/solution.py
@@ -259,7 +259,9 @@
     )
     up_act = jnp.dot(
         normed,
-        lax.all_gather(up_proj, "req", axis=0, tiled=True),
+        jnp.concatenate(
+            lax.all_to_all(jnp.stack([up_proj] * lax.axis_size("req")), "req", 0, 0), axis=0
+        ),
         preferred_element_type=jnp.float32,
     )
     latent_activation = (jax.nn.silu(gate_act) * up_act).astype(jnp.bfloat16)

time: 626 us -> 552 us (0.88)
  waiting for transfers between devices: 308 us -> 237 us
  loops' own time: 11.1 us -> 0.48 us
    all_gather x1 -> x0, waiting for transfers between devices: 63.6 us -> none  [body(): lax.all_gather(up_proj, 'req', axis=0, tiled=True)]
    another operation x1, loops' own time: 11.1 us -> 0.48 us  [entering(): return lax.fori_loop(0, devices, step, start)]
    psum x1, waiting for transfers between devices: 88.7 us -> 81.8 us  [body(): lax.psum(lax.dynamic_update_slice_in_dim(projected, own_part, offset, 1),...]
    unnamed x7 -> x6, waiting for transfers between devices: 39.8 us -> 39.3 us
    unnamed x51 -> x53, local copies, waits for them, and re-layouts: 16.2 us -> 16.2 us
  transfers between devices with their start and end apart: 12 -> 12, of which waited for: 5 -> 4; matrix products, arithmetic and copies ran while one was open for 10% -> 12% of each run, Pallas kernels for 0% -> 0%
where the time goes in v1:
time: 552 us; the launch traced here: 542 us
  waiting for transfers between devices  237 us (43%)
  matrix products  75 us (14%)
  blocking collectives  64.8 us (12%)
  other arithmetic  61.3 us (11%)
  local copies, waits for them, and re-layouts  58.2 us (11%)
  starting transfers between devices  29.9 us (5%)
  between operations  15.7 us (3%)
    psum x1, waiting for transfers between devices, body(): lax.psum(lax.dynamic_update_slice_in_dim(projected, own_part, offset, 1),...  81.8 us
    all_gather x1, waiting for transfers between devices, body(): lax.all_gather(gate_proj, 'req', axis=0, tiled=True)  60.6 us
    all_gather x1, waiting for transfers between devices, body(): lax.all_gather(down_proj, 'req', axis=1, tiled=True)  55.1 us
    unnamed x6, waiting for transfers between devices  39.3 us
    all_gather x1, blocking collectives, entering(): everything = jax.tree.map(lambda part: lax.all_gather(part, axis), x)  39.1 us
    select_n x16, other arithmetic, step(): return jax.tree.map(lambda a, b: jnp.where(reached, a, b), new, before)  32.6 us
    ppermute x6, starting transfers between devices, from_behind(): lax.ppermute(value, axis, [(source, source + steps) for source in range(l...  25 us
    dot_general x1, matrix products, block_contributions(): jnp.einsum('htu,uhp->thp', mixing * inner[group_index], driven, precision...  20.4 us
  transfers between devices with their start and end apart: 12, of which 4 were waited for; matrix products, arithmetic and copies ran while one was open for 12% of the time, Pallas kernels for 0%

profile of v1, /device:TPU:0, one launch (start us, length us, event | category | flops | bytes accessed | tf_op | source)
XLA Modules:
  0.0 542.2 jit_solution(3436221262910892269)
XLA Ops:
  8.7 3.6 collective-permute-start.3
  16.9 2.5 copy.75
  25.6 3.5 fusion.22
  29.2 5.4 collective-permute-start.2
  34.6 4.1 collective-permute-start.4
  38.7 4.3 collective-permute-start.5
  43.0 4.0 collective-permute-start
  47.0 3.6 collective-permute-start.1
  56.1 8.8 %gather_fusion = f32[14,512,512]{2,1,0:T(8,128)} fusion(f32[2,512,512]{2,1,0:T(8,128)} %fusion.59, s32[1024]{0:T(1024)} %copy-done.14), kind=kCustom, calls=%fused_computation | custom fusion | bytes 29360184 | tf_op jit(solution)/shard_map/gather | solution.py:85
  69.6 39.1 %all-gather.1 = f32[16,1,14]{2,1,0:T(1,128)S(1)} all-gather(f32[1,1,14]{2,1,0:T(1,128)S(1)} %bitcast.115), channel_id=1, replica_groups=mesh['req'=16,'mlp'=8] {'req'}, dimensions={0}, use_global_device_ids=true | all-gather | bytes 952 | tf_op jit(solution)/shard_map/all_gather | solution.py:26
  108.7 2.5 pad_maximum_fusion.1
  111.3 2.3 pad_maximum_fusion
  113.6 4.1 fusion.58
  117.7 6.2 %fusion.30 = bf16[2,224,512]{2,1,0:T(8,128)(2,1)} fusion(bf16[1536,2,224]{0,2,1:T(8,128)(2,1)} %bitcast.106, f32[2,512]{1,0:T(2,128)S(1)} %fusion.58, pred[512,1536]{0,1:T(8,128)(4,1)} %compare_and_fusion, bf16[1536,2,224]{0,2,1:T(8,128)(2,1)} %bitcast.105, bf16[512,2,224]{0,2,1:T(8,128)(2,1)} %bitcast.117), kind=kOutput, calls=%fused_computation.49 | convolution fusion | flops 1417382400 | bytes 4460544 | tf_op jit(solution)/shard_map/while/body/eval_jaxpr/hqk,khd->qhd/dot_general | solution.py:55
  123.9 33.2 %while.18 = (s32[]{:T(128)}, f32[14,64,64]{2,1,0:T(8,128)}, s32[]{:T(128)}, f32[16,14]{1,0:T(8,128)S(1)}, f32[16,14,64,64]{3,2,1,0:T(8,128)}, /*index=5*/s32[]{:T(128)}, s32[]{:T(128)}) while((s32[]{:T(128)}, f32[14,64,64]{2,1,0:T(8,128)}, s32[]{:T(128)}, f32[16,14]{1,0:T(8,128)S(1)}, f32[16,14,64,64]{3,2,1,0:T(8,128)}, ...), condition=%wide.region_5.6_spmd.clone, body=%wide.region_4.5_spmd.clone.sunk | while | flops 229380 | bytes 688401 | solution.py:36
  126.3 2.0 fusion.75
  128.3 2.0 fusion.75
  130.4 2.0 fusion.75
  132.4 2.0 fusion.75
  134.5 2.0 fusion.75
  136.6 2.0 fusion.75
  138.6 2.0 fusion.75
  140.7 2.0 fusion.75
  142.7 2.0 fusion.75
  157.1 2.3 fusion.37
  159.4 20.4 %fusion.21 = f32[512,14,64]{0,2,1:T(8,128)} fusion(f32[14,512,64]{1,2,0:T(8,128)S(1)} %fusion.37, f32[512,14,64]{0,2,1:T(8,128)S(1)} %bitcast.99, f32[14,512,512]{2,1,0:T(8,128)} %gather_fusion, f32[14,512]{1,0:T(8,128)S(1)} %bitcast.112, pred[512,512]{1,0:T(8,128)(4,1)S(1)} %copy-done.10, f32[14]{0:T(128)S(1)} %copy-done.19, f32[512,14]{0,1:T(8,128)S(1)} %copy-done.13, ...), kind=kOutput, calls=%fused_computation.38 | convolution fusion | flops 2831876096 | bytes 20533304 | tf_op jit(solution)/shard_map/htu,uhp->thp/dot_general | solution.py:84
  179.9 2.8 copy.80
  182.6 3.4 fusion.56
  186.1 2.8 copy.81
  190.5 12.4 %psum.21 = f32[512,2]{0,1:T(2,128)S(1)} all-reduce(f32[512,2]{0,1:T(2,128)S(1)} %reduce_sum.38), channel_id=1, replica_groups=mesh['req'=16,'mlp'=8] {'mlp'}, use_global_device_ids=true, to_apply=%region_7.8 | all-reduce | flops 1024 | bytes 8192 | tf_op jit(solution)/shard_map/psum | solution.py:235
  204.4 2.9 copy.82
  207.3 8.2 %fusion.35 = f32[512,3584]{1,0:T(8,128)S(1)} fusion(bf16[896,3584]{1,0:T(8,128)(2,1)} %param.38, f32[512,896]{1,0:T(8,128)} %copy.82, f32[896]{0:T(1024)S(1)} %copy-done.18, f32[512,896]{1,0:T(8,128)} %copy.80, bf16[512,896]{1,0:T(8,128)(2,1)} %param.30), kind=kOutput, calls=%fused_computation.57 | convolution fusion | flops 3292463104 | bytes 18353664 | tf_op jit(solution)/shard_map/dot_general | solution.py:243
  215.6 2.2 convolution_add_fusion
  217.8 3.0 copy-done.2
  221.1 5.8 %dynamic_update_slice.6 = f32[512,3584]{1,0:T(8,128)} dynamic-update-slice(f32[512,3584]{1,0:T(8,128)} %copy-done.2, f32[512,448]{1,0:T(8,128)S(1)} %convert_add_fusion, s32[]{:T(128)} %constant.100.clone.1, s32[]{:T(128)S(6)} %select_n.104) | dynamic-update-slice | bytes 1835012 | tf_op jit(solution)/shard_map/dynamic_update_slice | solution.py:251
  228.3 3.1 stack.4
  231.4 4.6 all-to-all-start
  236.1 81.8 %all-reduce.2.cloned.1.call-done = f32[512,3584]{1,0:T(8,128)} async-done(((f32[512,3584]{1,0:T(8,128)}), f32[512,3584]{1,0:T(8,128)}) %all-reduce.2.cloned.1.call-update) | async-done | bytes 7340048 | tf_op jit(solution)/shard_map/psum | solution.py:251
  317.9 3.6 multiply_reduce_fusion
  321.6 60.6 %all-gather.6.cloned.1.call-done = bf16[3584,896]{1,0:T(8,128)(2,1)} async-done(((bf16[224,896]{1,0:T(8,128)(2,1)}), bf16[3584,896]{1,0:T(8,128)(2,1)}) %all-gather.6.cloned.1.call-update) | async-done | bytes 6422544 | tf_op jit(solution)/shard_map/all_gather | solution.py:257
  382.2 8.5 %fusion.57 = f32[512,896]{1,0:T(8,128)S(1)} fusion(bf16[3584,896]{1,0:T(8,128)(2,1)} %all-gather.6.cloned.1.call-done, f32[512,3584]{1,0:T(8,128)} %all-reduce.2.cloned.1.call-done, f32[3584]{0:T(1024)S(1)} %copy-done.17, f32[512]{0:T(512)S(1)} %add_rsqrt_fusion.2), kind=kOutput, calls=%fused_computation.98 | convolution fusion | flops 3293839360 | bytes 15613952 | tf_op jit(solution)/shard_map/dot_general | solution.py:255
  390.6 55.1 %all-gather.8.cloned.1.call-done = bf16[896,3584]{0,1:T(8,128)(2,1)} async-done(((bf16[896,224]{0,1:T(8,128)(2,1)}), bf16[896,3584]{0,1:T(8,128)(2,1)}) %all-gather.8.cloned.1.call-update) | async-done | bytes 6422544 | tf_op jit(solution)/shard_map/all_gather | solution.py:270
  445.7 17.7 %convolution_bitcast_fusion = f32[3584,512]{1,0:T(8,128)} fusion(bf16[896,3584]{0,1:T(8,128)(2,1)} %all-gather.8.cloned.1.call-done, f32[512,896]{1,0:T(8,128)S(1)} %fusion.57, bf16[3584,896]{1,0:T(8,128)(2,1)} %bitcast.23, f32[512,3584]{1,0:T(8,128)} %all-reduce.2.cloned.1.call-done, f32[3584]{0:T(1024)S(1)} %copy-done.17, f32[512]{0:T(512)S(1)} %add_rsqrt_fusion.2), kind=kOutput, calls=%fused_computation.19 | convolution fusion | flops 6584926208 | bytes 29376512
  469.0 2.6 scatter_fusion
  472.6 38.0 %reduce-scatter.4.cloned.1.call-done = f32[448,512]{1,0:T(8,128)} async-done(((f32[3584,512]{1,0:T(8,128)}), f32[448,512]{1,0:T(8,128)}) %reduce-scatter.4.cloned.1.call-update) | async-done | bytes 917520
  510.6 2.7 copy.96
  513.3 2.8 fusion.31
  516.1 13.2 %psum.23 = f32[512]{0:T(512)S(1)} all-reduce(f32[512]{0:T(512)S(1)} %get-tuple-element.167), channel_id=1, replica_groups=mesh['req'=16,'mlp'=8] {'mlp'}, use_global_device_ids=true, to_apply=%region_12.13 | all-reduce | flops 512 | bytes 4096 | tf_op jit(solution)/shard_map/psum | solution.py:276
  (137 shorter events, 52.7 us)
Async XLA Ops:
  7.2 208.4 %copy-start = (bf16[448,3584]{1,0:T(8,128)(2,1)S(1)}, bf16[448,3584]{1,0:T(8,128)(2,1)}, u32[]{:S(2)}) copy-start(bf16[448,3584]{1,0:T(8,128)(2,1)} %param.37) | copy-start | bytes 9633796
  7.2 116.7 %all-gather.10.cloned.1.call-start = ((), (), s32[]{:S(2)}) async-start(), calls=%async_computation.5 | async-start | bytes 7798784 | tf_op jit(solution)/shard_map/all_gather | solution.py:26
  8.7 12.3 %collective-permute-start.3 = (s32[512]{0:T(512)}, s32[512]{0:T(512)S(1)}, u32[]{:S(2)}, u32[]{:S(2)}) collective-permute-start(s32[512]{0:T(512)} %broadcast_add_fusion.3), channel_id=1, source_target_pairs={{0,8},{8,16},{16,24},{24,32},{32,40},{40,48},{48,56},{56,64},{64,7... | collective-permute-start | bytes 6152 | tf_op jit(solution)/shard_map/ppermute | solution.py:21
  14.5 6.4 %copy-start.14 = (s32[1024]{0:T(1024)}, s32[1024]{0:T(1024)S(1)}, u32[]{:S(2)}) copy-start(s32[1024]{0:T(1024)S(1)} %pad_clamp_fusion) | copy-start | bytes 12292
  19.4 3.4 copy-start.12
  19.4 6.2 %copy-start.11 = (f32[512,14]{0,1:T(8,128)S(1)}, f32[512,14]{0,1:T(8,128)}, u32[]{:S(2)}) copy-start(f32[512,14]{0,1:T(8,128)} %param.33) | copy-start | bytes 86020
  29.1 288.8 %all-reduce.2.cloned.1.call-start = ((), (), s32[]{:S(2)}) async-start(), calls=%async_computation.2 | async-start | bytes 14680064 | tf_op jit(solution)/shard_map/psum | solution.py:251
  29.2 37.8 %collective-permute-start.2 = (s32[512]{0:T(512)}, s32[512]{0:T(512)}, u32[]{:S(2)}, u32[]{:S(2)}) collective-permute-start(s32[512]{0:T(512)} %broadcast_add_fusion.3), channel_id=1, source_target_pairs={{0,16},{8,24},{16,32},{24,40},{32,48},{40,56},{48,64},{56,72},{64,... | collective-permute-start | bytes 6152 | tf_op jit(solution)/shard_map/ppermute | solution.py:21
  34.6 74.2 %collective-permute-start.4 = (bf16[512,448]{0,1:T(8,128)(2,1)}, bf16[512,448]{0,1:T(8,128)(2,1)}, u32[]{:S(2)}, u32[]{:S(2)}) collective-permute-start(bf16[512,448]{0,1:T(8,128)(2,1)} %param.25), channel_id=1, source_target_pairs={{0,16},{8,24},{16,32},{24,40},{32,48},{40,56},{48,64},{56,72},{64,... | collective-permute-start | bytes 1376264 | tf_op jit(solution)/shard_map/ppermute | solution.py:21
  38.7 70.1 %collective-permute-start.5 = (bf16[512,448]{0,1:T(8,128)(2,1)}, bf16[512,448]{0,1:T(8,128)(2,1)}, u32[]{:S(2)}, u32[]{:S(2)}) collective-permute-start(bf16[512,448]{0,1:T(8,128)(2,1)} %param.25), channel_id=1, source_target_pairs={{0,8},{8,16},{16,24},{24,32},{32,40},{40,48},{48,56},{56,64},{64,7... | collective-permute-start | bytes 1376264 | tf_op jit(solution)/shard_map/ppermute | solution.py:21
  43.0 68.3 %collective-permute-start = (bf16[512,448]{0,1:T(8,128)(2,1)}, bf16[512,448]{0,1:T(8,128)(2,1)}, u32[]{:S(2)}, u32[]{:S(2)}) collective-permute-start(bf16[512,448]{0,1:T(8,128)(2,1)} %param.26), channel_id=1, source_target_pairs={{0,16},{8,24},{16,32},{24,40},{32,48},{40,56},{48,64},{56,72},{64,... | collective-permute-start | bytes 1376264 | tf_op jit(solution)/shard_map/ppermute | solution.py:21
  47.0 64.3 %collective-permute-start.1 = (bf16[512,448]{0,1:T(8,128)(2,1)}, bf16[512,448]{0,1:T(8,128)(2,1)}, u32[]{:S(2)}, u32[]{:S(2)}) collective-permute-start(bf16[512,448]{0,1:T(8,128)(2,1)} %param.26), channel_id=1, source_target_pairs={{0,8},{8,16},{16,24},{24,32},{32,40},{40,48},{48,56},{56,64},{64,7... | collective-permute-start | bytes 1376264 | tf_op jit(solution)/shard_map/ppermute | solution.py:21
  56.1 13.5 %copy-start.16 = (f32[14]{0:T(128)S(1)}, f32[14]{0:T(128)}, u32[]{:S(2)}) copy-start(f32[14]{0:T(128)} %get-tuple-element.156) | copy-start | bytes 172
  66.9 44.3 %copy-start.6 = (bf16[512,448]{0,1:T(8,128)(2,1)S(1)}, bf16[512,448]{0,1:T(8,128)(2,1)}, u32[]{:S(2)}) copy-start(bf16[512,448]{0,1:T(8,128)(2,1)} %param.26) | copy-start | bytes 1376260
  157.1 2.3 copy-start.3
  157.1 2.3 copy-start.10
  157.1 2.4 copy-start.13
  157.1 2.4 copy-start.19
  203.0 4.4 copy-start.18
  207.3 8.2 %copy-start.8 = (bf16[2,224,512]{2,1,0:T(8,128)(2,1)S(1)}, bf16[2,224,512]{2,1,0:T(8,128)(2,1)}, u32[]{:S(2)}) copy-start(bf16[2,224,512]{2,1,0:T(8,128)(2,1)} %fusion.30) | copy-start | bytes 1376260
  215.5 5.2 copy-start.4
  217.8 3.0 copy-start.2
  226.9 1.3 copy-start.9
  227.0 155.2 %all-gather.6.cloned.1.call-start = ((), (), s32[]{:S(2)}) async-start(), calls=%async_computation.3 | async-start | bytes 6823936 | tf_op jit(solution)/shard_map/all_gather | solution.py:257
  227.7 218.0 %all-gather.8.cloned.1.call-start = ((), (), s32[]{:S(2)}) async-start(), calls=%async_computation.4 | async-start | bytes 6823936 | tf_op jit(solution)/shard_map/all_gather | solution.py:270
  231.4 159.3 %all-to-all-start = ((bf16[16,224,896]{2,1,0:T(8,128)(2,1)}), bf16[16,224,896]{2,1,0:T(8,128)(2,1)}, u32[]{:S(2)}, u32[]{:S(2)}) async-start(bf16[16,224,896]{2,1,0:T(8,128)(2,1)} %stack.4), calls=%async_computation | async-start | bytes 12845056 | tf_op jit(solution)/shard_map/all_to_all | solution.py:263
  236.0 146.1 %copy-start.17 = (f32[3584]{0:T(1024)S(1)}, f32[3584]{0:T(1024)}, u32[]{:S(2)}) copy-start(f32[3584]{0:T(1024)} %param.39) | copy-start | bytes 43012
  236.1 274.6 %reduce-scatter.4.cloned.1.call-start = ((), (), s32[]{:S(2)}) async-start(), calls=%async_computation.6 | async-start | bytes 8257536
  463.5 1.0 copy-start.5
  463.5 1.2 copy-start.7
  466.5 2.0 copy-start.20
  510.6 20.8 %copy-start.15 = (f32[448]{0:T(512)S(1)}, f32[448]{0:T(512)}, u32[]{:S(2)}) copy-start(f32[448]{0:T(512)} %param.43) | copy-start | bytes 5380
  510.6 24.8 %copy-start.1 = (bf16[448,3584]{1,0:T(8,128)(2,1)S(1)}, bf16[448,3584]{1,0:T(8,128)(2,1)}, u32[]{:S(2)}) copy-start(bf16[448,3584]{1,0:T(8,128)(2,1)} %param.37) | copy-start | bytes 9633796
Sparse Core Ops, SparseCore 0:
  29.2 88.2 all-gather.9
  227.1 90.7 all-reduce.1
  320.1 62.0 all-gather.5
  384.1 61.5 all-gather.7
  463.6 46.9 reduce-scatter.3
